TPU v7x, 768 devices: a whole 4x8x12 slice. The times are simulated.
768 devices in a mesh: replica: 8 (over y), fsdp: 24 (over z_lo, x), tensor: 4 (over z_hi, core).
Axes of the slice: x: 4, y: 8, z: 12 (z_hi: 2, z_lo: 6; z = z_hi * 6 + z_lo), core: 2. Of those that a mesh axis runs over, the one named last changes fastest.
Arguments:
- tokens: bfloat16 [8, 192, 4096], P('replica', ('fsdp', 'tensor')), may hold values from -6 to 6
- d_out: bfloat16 [8, 192, 4096], P('replica', ('fsdp', 'tensor')), may hold values from -6 to 6
- w_gate: bfloat16 [4096, 15360], P(None, ('fsdp', 'tensor')), may hold values from -0.09375 to 0.09375
- w_up: bfloat16 [4096, 15360], P(None, ('fsdp', 'tensor')), may hold values from -0.09375 to 0.09375
- w_down: bfloat16 [15360, 4096], P(('fsdp', 'tensor')), may hold values from -0.046875 to 0.046875
- failed: int32 [96], P(('fsdp', 'tensor')), may hold values from 0 to 7
- master: float32 [2, 15360, 4096], P(None, ('fsdp', 'tensor'), 'replica'), may hold values from -6 to 6
- moment1: float32 [2, 15360, 4096], P(None, ('fsdp', 'tensor'), 'replica'), may hold values from -4 to 4
- moment2: float32 [2, 15360, 4096], P(None, ('fsdp', 'tensor'), 'replica'), may hold values from 0.1 to 1
Outputs:
- d_tokens: bfloat16 [8, 192, 4096], P('replica', ('fsdp', 'tensor'))
- master_new: float32 [15360, 4096], P(('fsdp', 'tensor'), 'replica')
- moment1_new: float32 [15360, 4096], P(('fsdp', 'tensor'), 'replica')
- moment2_new: float32 [15360, 4096], P(('fsdp', 'tensor'), 'replica')
All inputs are finite; a program needn't handle non-finite values.
Results may differ from a plain program's by a relative error of at most 0.0049.
Values may be sent and summed in bfloat16 or wider, within the bound.
A program may use at most 32 MiB of HBM per device.

v0:
```python
import jax
import jax.numpy as jnp
from jax import lax
from jax.sharding import PartitionSpec as P


def from_behind(block, axis, distance):
    devices = range(lax.axis_size(axis))
    route = [((i - distance) % len(devices), i) for i in devices]
    return lax.ppermute(block, axis, route)


def per_device(tokens, d_out, w_gate, w_up, w_down, failed, master, moment1, moment2):
    rows = tokens[0]
    grads_out = d_out[0]
    replicas = lax.axis_size("replica")
    row_piece = lax.all_gather(rows, ("fsdp", "tensor"), axis=0, tiled=True)
    out_piece = lax.all_gather(grads_out, ("fsdp", "tensor"), axis=0, tiled=True)
    gate = jnp.dot(row_piece, w_gate, preferred_element_type=jnp.float32)
    up = jnp.dot(row_piece, w_up, preferred_element_type=jnp.float32)
    sig = 1.0 / (1.0 + jnp.exp(-gate))
    hidden = (gate * sig * up).astype(jnp.bfloat16)
    d_hidden = lax.dot_general(
        out_piece, w_down, (((1,), (1,)), ((), ())), preferred_element_type=jnp.float32
    )
    d_gate = (d_hidden * up * sig * (1.0 + gate * (1.0 - sig))).astype(jnp.bfloat16)
    d_up = (d_hidden * gate * sig).astype(jnp.bfloat16)
    hidden, d_gate, d_up = (hidden, d_gate, d_up)
    grad_down = lax.dot_general(
        hidden, out_piece, (((0,), (0,)), ((), ())), preferred_element_type=jnp.float32
    )
    d_rows = lax.dot_general(
        d_gate, w_gate, (((1,), (1,)), ((), ())), preferred_element_type=jnp.float32
    )
    partial_value = d_rows + lax.dot_general(
        d_up, w_up, (((1,), (1,)), ((), ())), preferred_element_type=jnp.float32
    )
    folded = (grad_down, partial_value)
    grad_down = folded[0]
    d_rows = lax.psum_scatter(folded[1], ("fsdp", "tensor"), scatter_dimension=0, tiled=True)
    d_tokens = d_rows.astype(jnp.bfloat16)[None]
    failed_id = failed[0]
    own_index = lax.axis_index("replica")
    keep = (own_index != failed_id).astype(jnp.float32)
    grad = lax.psum_scatter(grad_down * keep, "replica", scatter_dimension=1, tiled=True) / (
        replicas - 1.0
    )
    backup = from_behind((master[1], moment1[1], moment2[1]), "replica", -1)
    lost = own_index == failed_id
    master_old = jnp.where(lost, backup[0], master[0])
    first_old = jnp.where(lost, backup[1], moment1[0])
    second_old = jnp.where(lost, backup[2], moment2[0])
    first_new = 0.9 * first_old + 0.1 * grad
    second_new = 0.95 * second_old + 0.05 * grad * grad
    master_new = master_old - 0.01 * first_new / (jnp.sqrt(second_new) + 1e-08)
    return (d_tokens, master_new, first_new, second_new)


def solution(mesh):
    placed = (
        P("replica", ("fsdp", "tensor"), None),
        P("replica", ("fsdp", "tensor"), None),
        P(None, ("fsdp", "tensor")),
        P(None, ("fsdp", "tensor")),
        P(("fsdp", "tensor"), None),
        P(("fsdp", "tensor")),
        P(None, ("fsdp", "tensor"), "replica"),
        P(None, ("fsdp", "tensor"), "replica"),
        P(None, ("fsdp", "tensor"), "replica"),
    )
    return jax.shard_map(
        per_device,
        mesh=mesh,
        in_specs=placed,
        out_specs=(
            P("replica", ("fsdp", "tensor"), None),
            P(("fsdp", "tensor"), "replica"),
            P(("fsdp", "tensor"), "replica"),
            P(("fsdp", "tensor"), "replica"),
        ),
        check_vma=False,
    )
```

profile of v0, /device:TPU:200, one launch (start us, length us, event | category | flops | bytes accessed | tf_op | source)
XLA Modules:
  0.0 1063.7 jit_solution(5516224008780314731)
XLA Ops:
  7.2 0.0 copy-start
  7.2 0.0 all-gather.7.cloned.1.call-start
  7.2 1.5 copy.16
  8.7 0.0 all-gather.7.cloned.1.call-update
  8.7 0.0 all-gather.5.cloned.1.call-start
  8.8 1.4 copy.15
  10.1 0.0 all-gather.5.cloned.1.call-update
  10.1 0.0 reduce-scatter.2.cloned.1.call-start
  10.8 0.0 copy-start.1
  10.9 176.6 %all-gather.7.cloned.1.call-done = bf16[1,192,4096]{2,0,1:T(2,128)(2,1)} async-done(((bf16[1,2,4096]{2,0,1:T(2,128)(2,1)}), bf16[1,192,4096]{2,0,1:T(2,128)(2,1)}) %all-gather.7.cloned.1.call-update) | async-done | bytes 1572880 | tf_op jit(solution)/shard_map/all_gather | solution.py:17
  187.4 0.0 copy-done
  187.4 3.8 fusion
  191.3 0.0 copy-done.1
  191.3 3.8 fusion.2
  195.1 166.6 %all-gather.5.cloned.1.call-done = bf16[1,192,4096]{2,0,1:T(2,128)(2,1)} async-done(((bf16[1,2,4096]{2,0,1:T(2,128)(2,1)}), bf16[1,192,4096]{2,0,1:T(2,128)(2,1)}) %all-gather.5.cloned.1.call-update) | async-done | bytes 1572880 | tf_op jit(solution)/shard_map/all_gather | solution.py:18
  361.7 5.4 convolution_multiply_fusion
  367.1 0.0 reduce-scatter.2.cloned.1.call-update
  367.2 1.7 slice_bitcast_fusion
  368.9 2.4 collective-permute-start.2
  371.3 1.7 slice_bitcast_fusion.1
  373.1 4.7 collective-permute-start.1
  377.8 1.7 slice_bitcast_fusion.2
  379.5 3.3 collective-permute-start
  382.9 1.3 dynamic-slice
  384.8 4.2 fusion.5
  389.0 0.6 fusion.16
  389.6 2.3 convolution_add_fusion
  391.9 0.0 copy-start.2
  391.9 662.2 %all-reduce.2 = bf16[192,4096]{1,0:T(8,128)(2,1)S(1)} all-reduce(f32[192,4096]{1,0:T(8,128)} %convolution_add_fusion), channel_id=4, replica_groups=mesh['replica'=8,'fsdp'=24,'tensor'=4] {'fsdp','tensor'}, use_global_device_ids=true, to_apply=%region_0.0.clone | all-reduce | flops 786432 | bytes 4718592
  1054.1 0.6 fusion.20
  1054.8 0.0 collective-permute-done.2
  1054.8 0.0 collective-permute-done.1
  1054.8 0.0 collective-permute-done
  1054.8 0.0 reduce-scatter.2.cloned.1.call-done
  1054.8 0.0 copy-done.2
  1054.8 2.3 fusion.15
Async XLA Ops:
  7.2 180.3 %copy-start = (bf16[4096,160]{0,1:T(8,128)(2,1)S(1)}, bf16[4096,160]{0,1:T(8,128)(2,1)}, u32[]{:S(2)}) copy-start(bf16[4096,160]{0,1:T(8,128)(2,1)} %param.11) | copy-start | bytes 3932164
  7.2 180.2 %all-gather.7.cloned.1.call-start = ((), (), s32[]{:S(2)}) async-start(), calls=%async_computation.3 | async-start | bytes 3178496 | tf_op jit(solution)/shard_map/all_gather | solution.py:17
  8.7 353.0 %all-gather.5.cloned.1.call-start = ((), (), s32[]{:S(2)}) async-start(), calls=%async_computation.2 | async-start | bytes 3178496 | tf_op jit(solution)/shard_map/all_gather | solution.py:18
  10.1 1044.7 %reduce-scatter.2.cloned.1.call-start = ((), (), s32[]{:S(2)}) async-start(), calls=%async_computation.1 | async-start | bytes 2949120 | tf_op jit(solution)/shard_map/reduce_scatter | solution.py:45
  10.8 180.4 %copy-start.1 = (bf16[4096,160]{0,1:T(8,128)(2,1)S(1)}, bf16[4096,160]{0,1:T(8,128)(2,1)}, u32[]{:S(2)}) copy-start(bf16[4096,160]{0,1:T(8,128)(2,1)} %param.12) | copy-start | bytes 3932164
  368.9 685.9 %collective-permute-start.2 = (f32[160,512]{1,0:T(8,128)}, f32[160,512]{1,0:T(8,128)}, u32[]{:S(2)}, u32[]{:S(2)}) collective-permute-start(f32[160,512]{1,0:T(8,128)} %slice_bitcast_fusion), channel_id=1, source_target_pairs={{96,0},{192,96},{288,192},{384,288},{480,384},{576,480},{672,576},... | collective-permute-start | bytes 983048 | tf_op jit(solution)/shard_map/ppermute | solution.py:10
  373.1 681.7 %collective-permute-start.1 = (f32[160,512]{1,0:T(8,128)}, f32[160,512]{1,0:T(8,128)}, u32[]{:S(2)}, u32[]{:S(2)}) collective-permute-start(f32[160,512]{1,0:T(8,128)} %slice_bitcast_fusion.1), channel_id=1, source_target_pairs={{96,0},{192,96},{288,192},{384,288},{480,384},{576,480},{672,576},... | collective-permute-start | bytes 983048 | tf_op jit(solution)/shard_map/ppermute | solution.py:10
  379.5 675.3 %collective-permute-start = (f32[160,512]{1,0:T(8,128)}, f32[160,512]{1,0:T(8,128)}, u32[]{:S(2)}, u32[]{:S(2)}) collective-permute-start(f32[160,512]{1,0:T(8,128)} %slice_bitcast_fusion.2), channel_id=1, source_target_pairs={{96,0},{192,96},{288,192},{384,288},{480,384},{576,480},{672,576},... | collective-permute-start | bytes 983048 | tf_op jit(solution)/shard_map/ppermute | solution.py:10
  391.9 662.9 %copy-start.2 = (f32[2,160,512]{2,1,0:T(8,128)S(1)}, f32[2,160,512]{2,1,0:T(8,128)}, u32[]{:S(2)}) copy-start(f32[2,160,512]{2,1,0:T(8,128)} %param.15) | copy-start | bytes 1966084
Sparse Core Ops, SparseCore 0:
  11.1 176.3 all-gather.6
  190.5 171.1 all-gather.4
  367.3 55.3 reduce-scatter.1
where the time goes:
time: 1060 us
  blocking collectives  662 us (62%)
  waiting for transfers between devices  343 us (32%)
  matrix products  20.2 us (2%)
  between operations  15.2 us (1%)
  starting transfers between devices  10.6 us (1%)
    unnamed x1, blocking collectives  662 us
    all_gather x1, waiting for transfers between devices, per_device(): row_piece = lax.all_gather(rows, ('fsdp', 'tensor'), axis=0, tiled=True)  177 us
    all_gather x1, waiting for transfers between devices, per_device(): lax.all_gather(grads_out, ('fsdp', 'tensor'), axis=0, tiled=True)  167 us
  transfers between devices with their start and end apart: 6, of which 2 were waited for; matrix products, arithmetic and copies ran while one was open for 2% of the time, Pallas kernels for 0%

commit v1 on v0

v1 whole, which is shorter than its diff:
```python
import functools

import jax
import jax.numpy as jnp
from jax import lax
from jax.experimental import pallas as pl
from jax.experimental.pallas import tpu as pltpu
from jax.sharding import PartitionSpec as P

MESH = pl.DeviceIdType.MESH
NX, NZ, NY = 4, 12, 8
ZH = 6
OFFS = (0, 1, 2, 3, -1, -2, -3, 4, 5, 6, -4, -5)
BF = jnp.bfloat16
F32 = jnp.float32
ROWS = 192
COLS = 512
FFD = 160
HALF = 80
GROUP = ((0, 112), (112, 80))
CHAINS = ((1, 0, 4), (-1, 1, 4), (1, 1, 3), (-1, 0, 3))
CHAIN_BASE = (0, 4, 8, 11)


def slot_of(off):
    off = (off + 5) % NZ - 5
    return OFFS.index(off)


def mod(a, n):
    return lax.rem(a + 2 * n, n)


def body(
    tok, dout, failed, wg_h, wu_h, wd_h, ma_h, m1_h, m2_h,
    dt_o, grad_o, bma_o, bm1_o, bm2_o,
    stage, recv8, tile, tokg, dog, wg, wu, wd, gsc, ysend, yrecv,
    sibs, sibr, acc, xsend, xrecv, zst, zrp, zrm, zsend, zfin, ostage, orecv,
    wsem, bs, br, as_, ar, zs, zr, gxs, gxr, gcs, gcr,
    ys, yr, cs, cr, xs, xr, ps, pr, fs, fr, os_, or_,
):
    y = lax.axis_index("replica")
    f = lax.axis_index("fsdp")
    t = lax.axis_index("tensor")
    x = lax.rem(f, NX)
    z = (t // 2) * ZH + f // NX
    c = lax.rem(t, 2)

    def dev(yy, xx, zz, cc):
        return (yy, lax.rem(zz, ZH) * NX + xx, (zz // ZH) * 2 + cc)

    def zpeer(k):
        return dev(y, x, mod(z + k, NZ), c)

    def xpeer(e):
        return dev(y, mod(x + e, NX), z, c)

    def ypeer(k):
        return dev(mod(y + k, NY), x, z, c)

    def gpeer(e, d):
        return dev(y, mod(x + e, NX), z, mod(c + d, 2))

    def jof(e, d):
        return mod(x + e, NX) * 2 + mod(c + d, 2)

    sib = dev(y, x, z, 1 - c)
    me = jof(0, 0)
    started = []

    def send(src, dst, ssem, rsem, peer):
        copy = pltpu.make_async_remote_copy(
            src_ref=src, dst_ref=dst, send_sem=ssem, recv_sem=rsem,
            device_id=peer, device_id_type=MESH,
        )
        copy.start()
        started.append(copy)

    def arrived(dst, ssem, rsem, peer):
        pltpu.make_async_remote_copy(
            src_ref=dst, dst_ref=dst, send_sem=ssem, recv_sem=rsem,
            device_id=peer, device_id_type=MESH,
        ).wait_recv()

    wcopies = [
        pltpu.make_async_copy(wg_h, wg, wsem.at[0]),
        pltpu.make_async_copy(wu_h, wu, wsem.at[1]),
    ] + [
        pltpu.make_async_copy(
            wd_h.at[:, pl.ds(COLS * j, COLS)], wd.at[j], wsem.at[2 + j]
        )
        for j in range(8)
    ]
    for copy in wcopies:
        copy.start()

    group8 = [(e, d) for e in (2, 1, 3, 0) for d in (0, 1) if (e, d) != (0, 0)]
    zoffs = (3, -3, 2, -2, 1, -1)
    barrier = pltpu.get_barrier_semaphore()
    greet = [gpeer(e, d) for e, d in group8]
    greet += [zpeer(k) for k in zoffs]
    greet += [ypeer(1), ypeer(-1)]
    for peer in greet:
        pl.semaphore_signal(barrier, inc=1, device_id=peer, device_id_type=MESH)
    for j in range(8):
        cols = pl.ds(COLS * j, COLS)
        stage[j, 0] = tok[0, :, cols]
        stage[j, 1] = dout[0, :, cols]
    recv8[me] = stage[me]
    pl.semaphore_wait(barrier, len(greet))

    def rel(e, d):
        return mod_static(-e, NX) * 2 + d

    def mod_static(a, n):
        return a % n

    for e, d in group8:
        send(
            stage.at[jof(e, d)], recv8.at[me],
            as_.at[e * 2 + d], ar.at[rel(e, d)], gpeer(e, d),
        )
    for i, (src, dst) in enumerate(((ma_h, bma_o), (m1_h, bm1_o), (m2_h, bm2_o))):
        send(src.at[1], dst, bs.at[i], br.at[i], ypeer(-1))
    for e, d in group8:
        arrived(recv8.at[jof(e, d)], as_.at[e * 2 + d], ar.at[e * 2 + d], gpeer(e, d))

    gathered = (tokg, dog)
    blk = lambda s: pl.ds(16 * s, 16)
    for i, g in enumerate(gathered):
        for j in range(8):
            tile[i, 2 * j : 2 * j + 2] = recv8[j, i].astype(F32)
        g[me, 0:16] = tile[i].astype(BF)
        for k in zoffs:
            s = slot_of(-k)
            send(g.at[me, blk(0)], g.at[me, blk(s)], zs.at[i, slot_of(k)], zr.at[i, s], zpeer(k))

    def zwait(i, off):
        s = slot_of(off)
        arrived(gathered[i].at[me, blk(s)], zs.at[i, s], zr.at[i, s], zpeer(1))

    for i, g in enumerate(gathered):
        zwait(i, -3)
        for n, k in enumerate((3, 2, 1)):
            s = slot_of(-3 - k)
            send(g.at[me, blk(slot_of(-3))], g.at[me, blk(s)], zs.at[i, 7 + n], zr.at[i, s], zpeer(k))
        zwait(i, 3)
        for n, k in enumerate((-2, -1)):
            s = slot_of(3 - k)
            send(g.at[me, blk(slot_of(3))], g.at[me, blk(s)], zs.at[i, 10 + n], zr.at[i, s], zpeer(k))

    def grp(q):
        return pl.ds(*GROUP[q])

    def to_sib(i, e, q):
        g = gathered[i]
        ref = g.at[jof(e, 0), grp(q)]
        send(ref, ref, gcs.at[i, e, q], gcr.at[i, e, q], sib)

    def from_sib(i, e, q):
        g = gathered[i]
        arrived(g.at[jof(e, 1), grp(q)], gcs.at[i, e, q], gcr.at[i, e, q], sib)

    def x_out(i, q):
        g = gathered[i]
        ref = g.at[me, grp(q)]
        for e in (2, 1, 3):
            send(ref, ref, gxs.at[i, e, q], gxr.at[i, (-e) % NX, q], xpeer(e))
        to_sib(i, 0, q)

    def x_in(i, e, q):
        g = gathered[i]
        arrived(g.at[jof(e, 0), grp(q)], gxs.at[i, e, q], gxr.at[i, e, q], xpeer(e))
        to_sib(i, e, q)

    for i in range(2):
        for off in (1, -1, 2, -2):
            zwait(i, off)
        x_out(i, 0)
        for off in (4, 5, 6, -4, -5):
            zwait(i, off)
        x_out(i, 1)

    wcopies[0].wait()
    wcopies[1].wait()

    def wrows(j):
        return pl.ds(pl.multiple_of(COLS * j, COLS), COLS)

    gate = jnp.zeros((ROWS, FFD), F32)
    up = jnp.zeros((ROWS, FFD), F32)

    def gate_up(gate, up, e, d):
        j = jof(e, d)
        a = tokg[j]
        gate = gate + jnp.dot(a, wg[wrows(j), :], preferred_element_type=F32)
        up = up + jnp.dot(a, wu[wrows(j), :], preferred_element_type=F32)
        return gate, up

    gate, up = gate_up(gate, up, 0, 0)
    for q in range(2):
        from_sib(0, 0, q)
    gate, up = gate_up(gate, up, 0, 1)
    for e in (1, 3, 2):
        for q in range(2):
            x_in(0, e, q)
        gate, up = gate_up(gate, up, e, 0)
    for e in (1, 3, 2):
        for q in range(2):
            from_sib(0, e, q)
        gate, up = gate_up(gate, up, e, 1)
    sig = 1.0 / (1.0 + jnp.exp(-gate))
    hidden = gate * sig * up
    hidden_t = hidden.T.astype(BF)

    for e in (1, 3, 2):
        for q in range(2):
            x_in(1, e, q)
    for e in (0, 1, 3, 2):
        for q in range(2):
            from_sib(1, e, q)

    keep = jnp.where(failed[0] == y, 0.0, 1.0).astype(F32)

    def grad_chunk(k):
        slab = mod(y + k, NY)
        gsc[k % NY] = jnp.dot(hidden_t, dog[slab], preferred_element_type=F32) * keep

    def half(h):
        return pl.ds(HALF * h, HALF)

    def y_hop(ci, h):
        s, ab, length = CHAINS[ci]
        n = CHAIN_BASE[ci] + h
        value = gsc[(s * (length - h)) % NY, half(ab)]
        if h > 0:
            arrived(yrecv.at[n - 1], ys.at[n - 1], yr.at[n - 1], ypeer(-s))
            value = value + yrecv[n - 1].astype(F32)
        ysend[n] = value.astype(BF)
        send(ysend.at[n], yrecv.at[n], ys.at[n], yr.at[n], ypeer(s))

    def y_step(h):
        for ci in range(4):
            if h < CHAINS[ci][2]:
                y_hop(ci, h)

    for k in (4, 3, -3):
        grad_chunk(k)
    y_step(0)

    for copy in wcopies[2:]:
        copy.wait()
    dh = jnp.zeros((ROWS, FFD), F32)
    for j in range(8):
        dh = dh + lax.dot_general(
            dog[j], wd[j], (((1,), (1,)), ((), ())), preferred_element_type=F32
        )
    d_gate = (dh * up * sig * (1.0 + gate * (1.0 - sig))).astype(BF)
    d_up = (dh * gate * sig).astype(BF)
    for k in (2, -2):
        grad_chunk(k)

    nt = (((1,), (1,)), ((), ()))

    def d_rows(e, d):
        j = jof(e, d)
        return lax.dot_general(d_gate, wg[wrows(j), :], nt, preferred_element_type=F32) + lax.dot_general(
            d_up, wu[wrows(j), :], nt, preferred_element_type=F32
        )

    order = (2, 1, 3, 0)

    def x_partial(e):
        arrived(sibr.at[e], cs.at[e], cr.at[e], sib)
        total = acc[e] + sibr[e].astype(F32)
        if e == 0:
            acc[0] = total
        else:
            xsend[e - 1] = total.astype(BF)
            send(
                xsend.at[e - 1, grp(1)], xrecv.at[(-e) % NX - 1, grp(1)],
                xs.at[e, 1], xr.at[(-e) % NX, 1], xpeer(e),
            )

    for n, e in enumerate(order):
        sibs[e] = d_rows(e, 1).astype(BF)
        send(sibs.at[e], sibr.at[e], cs.at[e], cr.at[e], sib)
        acc[e] = d_rows(e, 0)
        if n > 0:
            x_partial(order[n - 1])
        if n == 1:
            y_step(1)
    x_partial(0)
    for e in (2, 1, 3):
        send(
            xsend.at[e - 1, grp(0)], xrecv.at[(-e) % NX - 1, grp(0)],
            xs.at[e, 0], xr.at[(-e) % NX, 0], xpeer(e),
        )
    for k in (1, -1, 0):
        grad_chunk(k)
    y_step(2)

    for e in (2, 1, 3):
        arrived(xrecv.at[e - 1, grp(1)], xs.at[e, 1], xr.at[e, 1], xpeer(e))
    far = acc[0, grp(1)]
    for e in (2, 1, 3):
        far = far + xrecv[e - 1, grp(1)].astype(F32)
    zst[...] = far.astype(BF)
    send(zst.at[pl.ds(0, 48)], zrp, ps.at[0], pr.at[0], zpeer(3))
    send(zst.at[pl.ds(48, 32)], zrm, ps.at[1], pr.at[1], zpeer(-3))

    for e in (2, 1, 3):
        arrived(xrecv.at[e - 1, grp(0)], xs.at[e, 0], xr.at[e, 0], xpeer(e))
    near = acc[0, grp(0)]
    for e in (2, 1, 3):
        near = near + xrecv[e - 1, grp(0)].astype(F32)
    y_step(3)
    arrived(zrp, ps.at[0], pr.at[0], zpeer(-3))
    arrived(zrm, ps.at[1], pr.at[1], zpeer(3))
    for k in (3, -3, 2, -2, 1, -1):
        s = slot_of(k)
        value = near[16 * s : 16 * s + 16]
        if k > 0:
            value = value + zrp[16 * (k - 1) : 16 * k].astype(F32)
        elif k > -3:
            value = value + zrm[16 * (-k - 1) : 16 * -k].astype(F32)
        zsend[s - 1] = value.astype(BF)
        send(zsend.at[s - 1], zfin.at[slot_of(-k) - 1], fs.at[s - 1], fr.at[slot_of(-k) - 1], zpeer(k))
    total = near[0:16]
    for k in (1, -1, 2, -2, 3, -3):
        s = slot_of(k)
        arrived(zfin.at[s - 1], fs.at[s - 1], fr.at[s - 1], zpeer(k))
        total = total + zfin[s - 1].astype(F32)
    for j in range(8):
        ostage[j] = total[2 * j : 2 * j + 2].astype(BF)
    orecv[me] = ostage[me]
    for e, d in group8:
        send(
            ostage.at[jof(e, d)], orecv.at[me],
            os_.at[e * 2 + d], or_.at[rel(e, d)], gpeer(e, d),
        )

    for ci in range(4):
        s, ab, length = CHAINS[ci]
        n = CHAIN_BASE[ci] + length - 1
        arrived(yrecv.at[n], ys.at[n], yr.at[n], ypeer(-s))
    grad_o[half(0)] = gsc[0, half(0)] + yrecv[3].astype(F32) + yrecv[13].astype(F32)
    grad_o[half(1)] = gsc[0, half(1)] + yrecv[7].astype(F32) + yrecv[10].astype(F32)

    for e, d in group8:
        arrived(orecv.at[jof(e, d)], os_.at[e * 2 + d], or_.at[e * 2 + d], gpeer(e, d))
    for j in range(8):
        dt_o[:, pl.ds(COLS * j, COLS)] = orecv[j]
    for i, dst in enumerate((bma_o, bm1_o, bm2_o)):
        arrived(dst, bs.at[i], br.at[i], ypeer(1))
    for copy in started:
        copy.wait_send()


def exchange(tokens, d_out, failed, w_gate, w_up, w_down, master, moment1, moment2):
    vm = pl.BlockSpec(memory_space=pltpu.VMEM)
    sm = pl.BlockSpec(memory_space=pltpu.SMEM)
    anyw = pl.BlockSpec(memory_space=pl.ANY)
    state = jax.ShapeDtypeStruct((FFD, COLS), F32)
    sem = pltpu.SemaphoreType.DMA
    V = pltpu.VMEM
    return pl.pallas_call(
        body,
        out_shape=(jax.ShapeDtypeStruct((2, 4096), BF), state, state, state, state),
        in_specs=[vm, vm, sm, anyw, anyw, anyw, anyw, anyw, anyw],
        out_specs=(vm, vm, anyw, anyw, anyw),
        scratch_shapes=[
            V((8, 2, 2, COLS), BF), V((8, 2, 2, COLS), BF), V((2, 16, COLS), F32),
            V((8, ROWS, COLS), BF), V((8, ROWS, COLS), BF),
            V((4096, FFD), BF), V((4096, FFD), BF), V((8, FFD, COLS), BF),
            V((8, FFD, COLS), F32), V((14, HALF, COLS), BF), V((14, HALF, COLS), BF),
            V((4, ROWS, COLS), BF), V((4, ROWS, COLS), BF), V((4, ROWS, COLS), F32),
            V((3, ROWS, COLS), BF), V((3, ROWS, COLS), BF),
            V((80, COLS), BF), V((48, COLS), BF), V((32, COLS), BF),
            V((6, 16, COLS), BF), V((6, 16, COLS), BF),
            V((8, 2, COLS), BF), V((8, 2, COLS), BF),
            sem((10,)), sem((3,)), sem((3,)), sem((8,)), sem((8,)),
            sem((2, 12)), sem((2, 12)), sem((2, 4, 2)), sem((2, 4, 2)),
            sem((2, 4, 2)), sem((2, 4, 2)),
            sem((14,)), sem((14,)), sem((4,)), sem((4,)), sem((4, 2)), sem((4, 2)),
            sem((2,)), sem((2,)), sem((6,)), sem((6,)), sem((8,)), sem((8,)),
        ],
        compiler_params=pltpu.CompilerParams(
            collective_id=0, has_side_effects=True, vmem_limit_bytes=48 << 20
        ),
        name="exchange",
    )(tokens, d_out, failed, w_gate, w_up, w_down, master, moment1, moment2)


def per_device(tokens, d_out, w_gate, w_up, w_down, failed, master, moment1, moment2):
    d_tokens, total, back0, back1, back2 = exchange(
        tokens, d_out, failed, w_gate, w_up, w_down, master, moment1, moment2
    )
    grad = total / (lax.axis_size("replica") - 1.0)
    lost = lax.axis_index("replica") == failed[0]
    master_old = jnp.where(lost, back0, master[0])
    first_old = jnp.where(lost, back1, moment1[0])
    second_old = jnp.where(lost, back2, moment2[0])
    first_new = 0.9 * first_old + 0.1 * grad
    second_new = 0.95 * second_old + 0.05 * grad * grad
    master_new = master_old - 0.01 * first_new / (jnp.sqrt(second_new) + 1e-08)
    return (d_tokens[None], master_new, first_new, second_new)


def solution(mesh):
    placed = (
        P("replica", ("fsdp", "tensor"), None),
        P("replica", ("fsdp", "tensor"), None),
        P(None, ("fsdp", "tensor")),
        P(None, ("fsdp", "tensor")),
        P(("fsdp", "tensor"), None),
        P(("fsdp", "tensor")),
        P(None, ("fsdp", "tensor"), "replica"),
        P(None, ("fsdp", "tensor"), "replica"),
        P(None, ("fsdp", "tensor"), "replica"),
    )
    return jax.shard_map(
        per_device,
        mesh=mesh,
        in_specs=placed,
        out_specs=(
            P("replica", ("fsdp", "tensor"), None),
            P(("fsdp", "tensor"), "replica"),
            P(("fsdp", "tensor"), "replica"),
            P(("fsdp", "tensor"), "replica"),
        ),
        check_vma=False,
    )
```

time: 1060 us -> 92.8 us (0.09)
  the two profiles are of different devices: /device:TPU:200 before, /device:TPU:1 now
where the time goes in v1:
time: 92.8 us; the launch traced here: 92.7 us
  Pallas kernels  77.8 us (84%)
  local copies, waits for them, and re-layouts  11.1 us (12%)
  other arithmetic  2.4 us (3%)
  between operations  1.35 us (1%)
    pallas_call x1, Pallas kernels, exchange(): pl.pallas_call(body, out_shape=(jax.ShapeDtypeStruct((2, 4096), BF), stat...  77.8 us
    unnamed x23, local copies, waits for them, and re-layouts  11.1 us
    sub x1, other arithmetic, per_device(): master_new = master_old - 0.01 * first_new / (jnp.sqrt(second_new) + 1e-08)  2.4 us

profile of v1, /device:TPU:1, one launch (start us, length us, event | category | flops | bytes accessed | tf_op | source)
XLA Modules:
  0.0 92.7 jit_solution(7152805080637370842)
XLA Ops:
  1.3 3.7 %copy.13.wg_h = bf16[4096,160]{1,0:T(8,128)(2,1)} copy(bf16[4096,160]{0,1:T(8,128)(2,1)} %param.11) | data formatting | bytes 2621440 | tf_op args[2]
  5.0 0.0 copy-start
  5.0 0.0 copy-start.1
  5.0 0.0 copy-start.2
  5.0 0.0 copy-start.3
  5.0 0.0 copy-start.8
  5.0 0.0 copy-start.9
  5.0 3.9 %copy.14.wu_h = bf16[4096,160]{1,0:T(8,128)(2,1)} copy(bf16[4096,160]{0,1:T(8,128)(2,1)} %param.12) | data formatting | bytes 2621440 | tf_op args[3]
  8.9 0.0 copy-done
  8.9 0.0 copy-done.1
  8.9 0.0 copy-done.2
  8.9 0.0 copy-done.3
  8.9 0.0 copy-done.8
  8.9 0.0 copy-done.9
  8.9 77.8 %exchange.1 = (bf16[2,4096]{1,0:T(2,128)(2,1)S(1)}, f32[160,512]{1,0:T(8,128)S(1)}, f32[160,512]{1,0:T(8,128)S(1)}, f32[160,512]{1,0:T(8,128)S(1)}, f32[160,512]{1,0:T(8,128)S(1)}) custom-call(bf16[1,2,4096]{2,1,0:T(2,128)(2,1)S(1)} %copy-done.8, bf16[1,2,4096]{2,1,0:T(2,128)(2,1)S(1)} %copy-done.9, s32[1]{0:T(128)} %copy.16.failed, ...), custom_call_target="tpu_custom_call" | custom-call | tf_op jit(solution)/shard_map/exchange/pallas_call | solution.py:367
  86.8 0.0 copy-start.4
  86.8 0.7 copy-done.4
  87.5 0.0 copy-start.5
  87.5 0.7 copy-done.5
  88.2 0.0 copy-start.6
  88.2 0.7 copy-done.6
  88.9 0.0 copy-start.7
  88.9 0.7 copy-done.7
  89.7 2.4 %fusion.4 = (f32[160,512]{1,0:T(8,128)}, f32[160,512]{1,0:T(8,128)}, f32[160,512]{1,0:T(8,128)}) fusion(f32[160,512]{1,0:T(8,128)} %copy-done.5, f32[2,160,512]{2,1,0:T(8,128)S(1)} %copy-done, pred[]{:T(512)S(6)} %eq.3, f32[160,512]{1,0:T(8,128)} %copy-done.4, f32[160,512]{1,0:T(8,128)} %copy-done.6, f32[2,160,512]{2,1,0:T(8,128)S(1)} %copy-done.1, ...), kind=kLoop, calls=%fused_computation.7 | loop fusion | flops 1228800 | bytes 3276801 | tf_op jit(solution)/shard_map/sub | solution.py:406
  92.1 0.6 copy.17
Async XLA Ops:
  5.0 3.9 %copy-start = (f32[2,160,512]{2,1,0:T(8,128)S(1)}, f32[2,160,512]{2,1,0:T(8,128)}, u32[]{:S(2)}) copy-start(f32[2,160,512]{2,1,0:T(8,128)} %ma_h.1) | copy-start | bytes 1966084
  5.0 3.9 %copy-start.1 = (f32[2,160,512]{2,1,0:T(8,128)S(1)}, f32[2,160,512]{2,1,0:T(8,128)}, u32[]{:S(2)}) copy-start(f32[2,160,512]{2,1,0:T(8,128)} %m1_h.1) | copy-start | bytes 1966084
  5.0 3.9 %copy-start.2 = (f32[2,160,512]{2,1,0:T(8,128)S(1)}, f32[2,160,512]{2,1,0:T(8,128)}, u32[]{:S(2)}) copy-start(f32[2,160,512]{2,1,0:T(8,128)} %m2_h.1) | copy-start | bytes 1966084
  5.0 3.9 %copy-start.3 = (bf16[160,4096]{1,0:T(8,128)(2,1)S(1)}, bf16[160,4096]{1,0:T(8,128)(2,1)}, u32[]{:S(2)}) copy-start(bf16[160,4096]{1,0:T(8,128)(2,1)} %wd_h.1) | copy-start | bytes 3932164
  5.0 3.9 %copy-start.8 = (bf16[1,2,4096]{2,1,0:T(2,128)(2,1)S(1)}, bf16[1,2,4096]{2,1,0:T(2,128)(2,1)}, u32[]{:S(2)}) copy-start(bf16[1,2,4096]{2,1,0:T(2,128)(2,1)} %tok.1) | copy-start | bytes 49156
  5.0 3.9 %copy-start.9 = (bf16[1,2,4096]{2,1,0:T(2,128)(2,1)S(1)}, bf16[1,2,4096]{2,1,0:T(2,128)(2,1)}, u32[]{:S(2)}) copy-start(bf16[1,2,4096]{2,1,0:T(2,128)(2,1)} %dout.1) | copy-start | bytes 49156
  86.8 0.7 copy-start.4
  87.5 0.7 copy-start.5
  88.2 0.7 copy-start.6
  88.9 0.7 copy-start.7
